TPU v7x, 256 devices: a whole 4x4x8 slice. The times are simulated.
256 devices in a mesh: dp: 8 (over z_lo, core), mp: 16 (over x, y), group: 2 (over z_hi).
Axes of the slice: x: 4, y: 4, z: 8 (z_hi: 2, z_lo: 4; z = z_hi * 4 + z_lo), core: 2. Of those that a mesh axis runs over, the one named last changes fastest.
Arguments:
- hidden: bfloat16 [1024, 8192], P('dp', 'mp'), may hold values from -6 to 6
- neighbour_ids: int32 [16, 2, 128], P('dp', 'group'), may hold values from 0 to 65535, as said below
- counts: int32 [16], P('dp'), may hold values from 0 to 2
- embed_table: bfloat16 [65536, 8192], P(('dp', 'group'), 'mp'), may hold values from -6 to 6
- w_query: bfloat16 [8192, 4096], P('group', 'mp'), may hold values from -0.0625 to 0.0625
- w_key: bfloat16 [8192, 4096], P('group', 'mp'), may hold values from -0.0625 to 0.0625
- w_value: bfloat16 [8192, 4096], P('group', 'mp'), may hold values from -0.0625 to 0.0625
- w_out: bfloat16 [4096, 8192], P('mp', 'group'), may hold values from -0.09375 to 0.09375
- grad_out: bfloat16 [1024, 8192], P('dp', 'mp'), may hold values from -6 to 6
Outputs:
- output: float32 [1024, 8192], P('dp', 'mp')
- grad_hidden: float32 [1024, 8192], P('dp', 'mp')
- grad_neighbours: float32 [16, 2, 128, 8192], P('dp', 'group', None, 'mp')
Inputs may be any that keep to these rules, and one draw needn't show every extreme that they name: `neighbour_ids`: token ids of the retrieved neighbours; the ids are split into 16 owners of 4096 consecutive ids each; of the 256 ids of one window's neighbour k (blocks of one window, one k), at most 64 belong to one owner, and exactly 64 belong to some owner. neighbours k < counts[c] of block c are used, the others are masked.
All inputs are finite; a program needn't handle non-finite values.
Results may differ from a plain program's by a relative error of at most 0.019.
Values may be sent and summed in bfloat16 or wider, within the bound.
A program may use at most 128 MiB of HBM per device.

v0:
```python
import math
import jax
import jax.numpy as jnp
from jax import lax
from jax.sharding import PartitionSpec as P

HD = 128
BLOCK = 64
RET = 128


def contract(left, right):
    return lax.dot_general(
        left, right, (((1,), (1,)), ((), ())), preferred_element_type=jnp.float32
    )


def per_device(
    hidden, neighbour_ids, counts, embed_table, w_query, w_key, w_value, w_out, grad_out
):
    tail_rows = BLOCK - 1
    rows_here = hidden.shape[0]
    blocks_here = rows_here // BLOCK
    heads_here = w_query.shape[1] // HD
    inv_root = 1.0 / math.sqrt(HD)
    keep_rows = rows_here - tail_rows
    pad_rows = jnp.zeros((tail_rows, hidden.shape[1]), jnp.bfloat16)
    query_rows = jnp.concatenate([hidden[tail_rows:], pad_rows], 0)
    grad_rows = jnp.concatenate([grad_out[tail_rows:], pad_rows], 0)
    full_query, full_grad = (
        lax.all_gather(query_rows, "mp", axis=1, tiled=True),
        lax.all_gather(grad_rows, "mp", axis=1, tiled=True),
    )
    flat_ids = neighbour_ids.reshape(-1)
    block_rows = embed_table.shape[0]
    owners = lax.axis_size("dp") * lax.axis_size("group")
    cap = flat_ids.shape[0] // 4
    every_id = (
        lax.all_gather(flat_ids.astype(jnp.float32), ("dp", "group"), axis=0, tiled=True)
        .astype(jnp.int32)
        .reshape(owners, -1)
    )
    owner = lax.axis_index("dp") * lax.axis_size("group") + lax.axis_index("group")
    local_ids = every_id - owner * block_rows
    inside = (local_ids >= 0) & (local_ids < block_rows)
    rank = jnp.cumsum(inside.astype(jnp.int32), axis=1) - 1
    slot_hit = inside[:, :, None] & (rank[:, :, None] == jnp.arange(cap)[None, None, :])
    send_rows = jnp.sum(jnp.where(slot_hit, local_ids[:, :, None], 0), axis=1)
    send_buf = embed_table[send_rows.reshape(-1)].reshape(owners, cap, -1)
    recv_buf = lax.all_to_all(send_buf, ("dp", "group"), 0, 0, tiled=True)
    own_owner = flat_ids // block_rows
    same_owner = own_owner[:, None] == jnp.arange(owners)[None, :]
    own_rank = (
        jnp.sum(jnp.where(same_owner, jnp.cumsum(same_owner.astype(jnp.int32), axis=0), 0), axis=1)
        - 1
    )
    own_cols = recv_buf.reshape(owners * cap, -1)[own_owner * cap + own_rank]
    neighbours = lax.all_gather(own_cols, "mp", axis=1, tiled=True)
    wq_full, wk_full, wv_full = (
        lax.all_gather(w_query, "group", axis=0, tiled=True),
        lax.all_gather(w_key, "group", axis=0, tiled=True),
        lax.all_gather(w_value, "group", axis=0, tiled=True),
    )
    query_sum = jnp.dot(full_query, wq_full, preferred_element_type=jnp.float32)
    query = query_sum.astype(jnp.bfloat16)
    wo_full = lax.all_gather(w_out, "group", axis=1, tiled=True)
    keys = jnp.dot(neighbours, wk_full, preferred_element_type=jnp.float32).astype(jnp.bfloat16)
    values = jnp.dot(neighbours, wv_full, preferred_element_type=jnp.float32).astype(jnp.bfloat16)
    key_block = keys.reshape(blocks_here, RET, heads_here, HD)
    value_block = values.reshape(blocks_here, RET, heads_here, HD)
    query_block = query.reshape(blocks_here, BLOCK, heads_here, HD)
    live = (counts > lax.axis_index("group")).astype(jnp.float32)
    scores = (
        jnp.einsum("cqhd,ckhd->chqk", query_block, key_block, preferred_element_type=jnp.float32)
        * inv_root
    )
    weights = jnp.exp(scores) * live[:, None, None, None]
    numer = jnp.einsum(
        "chqk,ckhd->cqhd",
        weights.astype(jnp.bfloat16),
        value_block,
        preferred_element_type=jnp.float32,
    )
    partial_total = jnp.sum(weights, -1)
    numer, partial_total = lax.psum((numer, partial_total), "group")
    total = partial_total + 1.0
    attn = numer / jnp.transpose(total, (0, 2, 1))[..., None]
    attn_bf = attn.reshape(rows_here, heads_here * HD).astype(jnp.bfloat16)
    out_term = jnp.dot(attn_bf, wo_full, preferred_element_type=jnp.float32)
    d_attn = contract(full_grad, wo_full).astype(jnp.bfloat16)
    d_block = d_attn.reshape(blocks_here, BLOCK, heads_here, HD)
    prob = weights / total[..., None]
    d_prob = jnp.einsum("cqhd,ckhd->chqk", d_block, value_block, preferred_element_type=jnp.float32)
    delta = jnp.sum(d_block.astype(jnp.float32) * attn, -1)
    d_score = (prob * (d_prob - jnp.transpose(delta, (0, 2, 1))[..., None])).astype(jnp.bfloat16)
    query_part = jnp.einsum(
        "chqk,ckhd->cqhd", d_score, key_block, preferred_element_type=jnp.float32
    )
    query_grad = lax.psum(query_part, "group")
    d_query = (query_grad * inv_root).astype(jnp.bfloat16).reshape(rows_here, heads_here * HD)
    d_keys = (
        jnp.einsum("chqk,cqhd->ckhd", d_score, query_block, preferred_element_type=jnp.float32)
        * inv_root
    ).astype(jnp.bfloat16)
    d_values = jnp.einsum(
        "chqk,cqhd->ckhd", prob.astype(jnp.bfloat16), d_block, preferred_element_type=jnp.float32
    ).astype(jnp.bfloat16)
    d_keys = d_keys.reshape(blocks_here * RET, heads_here * HD)
    d_values = d_values.reshape(blocks_here * RET, heads_here * HD)
    hid_term = contract(d_query, wq_full)
    out_cols, hid_cols = (
        lax.psum_scatter(
            out_term.astype(jnp.bfloat16), "mp", scatter_dimension=1, tiled=True
        ).astype(jnp.float32),
        lax.psum_scatter(
            hid_term.astype(jnp.bfloat16), "mp", scatter_dimension=1, tiled=True
        ).astype(jnp.float32),
    )
    zero_rows = jnp.zeros((tail_rows, out_cols.shape[1]), jnp.float32)
    output = jnp.concatenate([zero_rows, out_cols[:keep_rows]], 0)
    grad_hidden = jnp.concatenate([zero_rows, hid_cols[:keep_rows]], 0)
    neigh_term = contract(d_keys, wk_full) + contract(d_values, wv_full)
    neigh_cols = lax.psum_scatter(
        neigh_term.astype(jnp.bfloat16), "mp", scatter_dimension=1, tiled=True
    ).astype(jnp.float32)
    grad_neighbours = neigh_cols.reshape(blocks_here, 1, RET, neigh_cols.shape[1])
    return (output, grad_hidden, grad_neighbours)


def solution(mesh):
    return jax.shard_map(
        per_device,
        mesh=mesh,
        in_specs=(
            P("dp", "mp"),
            P("dp", "group", None),
            P("dp"),
            P(("dp", "group"), "mp"),
            P("group", "mp"),
            P("group", "mp"),
            P("group", "mp"),
            P("mp", "group"),
            P("dp", "mp"),
        ),
        out_specs=(P("dp", "mp"), P("dp", "mp"), P("dp", "group", None, "mp")),
        check_vma=False,
    )
```

profile of v0, /device:TPU:2, one launch (start us, length us, event | category | flops | bytes accessed | tf_op | source)
XLA Modules:
  0.0 972.8 jit_solution(12286093274936307989)
XLA Ops:
  7.2 0.9 slice.30
  8.1 0.7 concatenate.16
  8.9 0.7 all-gather.14.cloned.1.call-update
  9.6 0.9 slice.32
  10.5 0.7 concatenate.19
  11.3 0.5 all-gather.18.cloned.1.call-update
  11.8 0.5 all-gather.10.cloned.1.call-update
  12.4 40.9 %all-gather.1 = f32[16,1,256]{2,1,0:T(1,128)S(1)} all-gather(f32[1,1,256]{2,1,0:T(1,128)S(1)} %bitcast.107), channel_id=1, replica_groups=mesh['dp'=8,'mp'=16,'group'=2] {'dp','group'}, dimensions={0}, use_global_device_ids=true | all-gather | bytes 17408 | tf_op jit(solution)/shard_map/all_gather | solution.py:39
  53.5 0.6 reduce-window.14
  54.4 0.4 select_reduce_fusion
  54.8 7.9 gather_fusion
  62.7 6.0 all-to-all-start
  68.8 0.6 reduce-window.16
  69.8 38.2 %all-to-all-done = bf16[16,64,512]{2,1,0:T(8,128)(2,1)S(1)} async-done(((bf16[16,64,512]{2,1,0:T(8,128)(2,1)}), bf16[16,64,512]{2,1,0:T(8,128)(2,1)S(1)}, u32[]{:S(2)}, u32[]{:S(2)}) %all-to-all-start) | async-done | bytes 1048608 | tf_op jit(solution)/shard_map/all_to_all | solution.py:50
  107.9 1.9 gather_fusion.1
  109.9 0.7 all-gather.16.cloned.1.call-update
  110.7 60.2 %all-gather.14.cloned.1.call-done = bf16[8192,256]{1,0:T(8,128)(2,1)} async-done(((bf16[4096,256]{1,0:T(8,128)(2,1)}), bf16[8192,256]{1,0:T(8,128)(2,1)}) %all-gather.14.cloned.1.call-update) | async-done | bytes 4194320 | tf_op jit(solution)/shard_map/all_gather | solution.py:60
  170.9 3.5 convolution_convert_fusion.6
  174.4 65.6 %all-gather.20.cloned.1.call-done = bf16[128,8192]{1,0:T(8,128)(2,1)} async-done(((bf16[128,512]{1,0:T(8,128)(2,1)}), bf16[128,8192]{1,0:T(8,128)(2,1)}) %all-gather.20.cloned.1.call-update) | async-done | bytes 2097168 | tf_op jit(solution)/shard_map/all_gather | solution.py:32
  240.0 113.4 %all-gather.18.cloned.1.call-done = bf16[256,8192]{1,0:T(8,128)(2,1)} async-done(((bf16[256,4096]{1,0:T(8,128)(2,1)}), bf16[256,8192]{1,0:T(8,128)(2,1)}) %all-gather.18.cloned.1.call-update) | async-done | bytes 4194320 | tf_op jit(solution)/shard_map/all_gather | solution.py:66
  353.4 4.4 convolution_convert_fusion.5
  357.8 105.4 %all-gather.10.cloned.1.call-done = bf16[8192,256]{1,0:T(8,128)(2,1)} async-done(((bf16[4096,256]{1,0:T(8,128)(2,1)}), bf16[8192,256]{1,0:T(8,128)(2,1)}) %all-gather.10.cloned.1.call-update) | async-done | bytes 4194320 | tf_op jit(solution)/shard_map/all_gather | solution.py:62
  463.2 61.3 %all-gather.22.cloned.1.call-done = bf16[256,8192]{1,0:T(8,128)(2,1)} async-done(((bf16[256,512]{1,0:T(8,128)(2,1)}), bf16[256,8192]{1,0:T(8,128)(2,1)}) %all-gather.22.cloned.1.call-update) | async-done | bytes 4194320 | tf_op jit(solution)/shard_map/all_gather | solution.py:58
  524.5 4.7 convolution_convert_fusion.4
  529.2 108.8 %all-gather.16.cloned.1.call-done = bf16[8192,256]{1,0:T(8,128)(2,1)} async-done(((bf16[4096,256]{1,0:T(8,128)(2,1)}), bf16[8192,256]{1,0:T(8,128)(2,1)}) %all-gather.16.cloned.1.call-update) | async-done | bytes 4194320 | tf_op jit(solution)/shard_map/all_gather | solution.py:61
  638.1 4.7 convolution_convert_fusion.3
  642.8 0.3 fusion.33
  643.1 0.8 convolution_bitcast_fusion.1
  644.0 8.8 psum.22
  652.9 25.8 %all-reduce.7.cloned.1.call-done = f32[2,64,2,128]{3,1,2,0:T(8,128)} async-done(((f32[2,64,2,128]{3,1,2,0:T(8,128)}), f32[2,64,2,128]{3,1,2,0:T(8,128)}) %all-reduce.7.cloned.1.call-update) | async-done | bytes 131088 | tf_op jit(solution)/shard_map/psum | solution.py:85
  678.7 1.1 multiply_reduce_fusion
  680.1 0.8 convolution_bitcast_fusion
  681.0 4.3 convolution_convert_fusion.1
  685.3 31.5 %all-reduce.9.cloned.1.call-done = f32[2,64,2,128]{3,1,2,0:T(8,128)} async-done(((f32[2,64,2,128]{3,1,2,0:T(8,128)}), f32[2,64,2,128]{3,1,2,0:T(8,128)}) %all-reduce.9.cloned.1.call-update) | async-done | bytes 131088 | tf_op jit(solution)/shard_map/psum | solution.py:99
  716.9 0.9 multiply_convert_fusion
  717.9 5.0 convolution_convert_fusion
  723.1 0.3 fusion.3
  723.6 0.2 fusion.2
  724.0 3.6 fusion.11
  727.6 3.2 fusion
  730.8 64.9 %reduce-scatter.4.cloned.1.call-done = bf16[128,512]{1,0:T(8,128)(2,1)} async-done(((bf16[128,8192]{1,0:T(8,128)(2,1)}), bf16[128,512]{1,0:T(8,128)(2,1)}) %reduce-scatter.4.cloned.1.call-update) | async-done | bytes 131088 | tf_op jit(solution)/shard_map/reduce_scatter | solution.py:112
  795.7 0.9 slice.40
  796.6 0.7 pad_convert_fusion.1
  797.3 81.1 %reduce-scatter.6.cloned.1.call-done = bf16[128,512]{1,0:T(8,128)(2,1)} async-done(((bf16[128,8192]{1,0:T(8,128)(2,1)}), bf16[128,512]{1,0:T(8,128)(2,1)}) %reduce-scatter.6.cloned.1.call-update) | async-done | bytes 131088 | tf_op jit(solution)/shard_map/reduce_scatter | solution.py:115
  878.5 0.9 slice.41
  879.3 0.7 pad_convert_fusion
  880.1 84.0 %reduce-scatter.8.cloned.1.call-done = bf16[256,512]{1,0:T(8,128)(2,1)} async-done(((bf16[256,8192]{1,0:T(8,128)(2,1)}), bf16[256,512]{1,0:T(8,128)(2,1)}) %reduce-scatter.8.cloned.1.call-update) | async-done | bytes 262160 | tf_op jit(solution)/shard_map/reduce_scatter | solution.py:123
  964.1 1.8 convert.9
  (62 shorter events, 2.4 us)
Async XLA Ops:
  7.2 5.2 copy-start.1
  7.2 103.5 %all-gather.12.cloned.1.call-start = ((), (), s32[]{:S(2)}) async-start(), calls=%async_computation.5 | async-start | bytes 2228224 | tf_op jit(solution)/shard_map/all_gather | solution.py:31
  8.8 162.1 %all-gather.14.cloned.1.call-start = ((), (), s32[]{:S(2)}) async-start(), calls=%async_computation.6 | async-start | bytes 6291456 | tf_op jit(solution)/shard_map/all_gather | solution.py:60
  9.6 230.4 %all-gather.20.cloned.1.call-start = ((), (), s32[]{:S(2)}) async-start(), calls=%async_computation.11 | async-start | bytes 2228224 | tf_op jit(solution)/shard_map/all_gather | solution.py:32
  11.2 342.2 %all-gather.18.cloned.1.call-start = ((), (), s32[]{:S(2)}) async-start(), calls=%async_computation.9 | async-start | bytes 6291456 | tf_op jit(solution)/shard_map/all_gather | solution.py:66
  11.8 451.4 %all-gather.10.cloned.1.call-start = ((), (), s32[]{:S(2)}) async-start(), calls=%async_computation.4 | async-start | bytes 6291456 | tf_op jit(solution)/shard_map/all_gather | solution.py:62
  62.7 47.9 %copy-start.2 = (s32[2]{0:T(128)S(1)}, s32[2]{0:T(128)}, u32[]{:S(2)}) copy-start(s32[2]{0:T(128)} %param.11) | copy-start | bytes 28
  62.7 45.2 %all-to-all-start = ((bf16[16,64,512]{2,1,0:T(8,128)(2,1)}), bf16[16,64,512]{2,1,0:T(8,128)(2,1)S(1)}, u32[]{:S(2)}, u32[]{:S(2)}) async-start(bf16[16,64,512]{2,1,0:T(8,128)(2,1)} %bitcast.4), calls=%async_computation | async-start | bytes 2097152 | tf_op jit(solution)/shard_map/all_to_all | solution.py:50
  68.7 455.8 %all-gather.22.cloned.1.call-start = ((), (), s32[]{:S(2)}) async-start(), calls=%async_computation.15 | async-start | bytes 4456448 | tf_op jit(solution)/shard_map/all_gather | solution.py:58
  109.8 528.2 %all-gather.16.cloned.1.call-start = ((), (), s32[]{:S(2)}) async-start(), calls=%async_computation.7 | async-start | bytes 6291456 | tf_op jit(solution)/shard_map/all_gather | solution.py:61
  110.6 568.1 %all-reduce.7.cloned.1.call-start = ((), (), s32[]{:S(2)}) async-start(), calls=%async_computation.8 | async-start | bytes 262144 | tf_op jit(solution)/shard_map/psum | solution.py:85
  644.0 72.9 %all-reduce.9.cloned.1.call-start = ((), (), s32[]{:S(2)}) async-start(), calls=%async_computation.12 | async-start | bytes 262144 | tf_op jit(solution)/shard_map/psum | solution.py:99
  680.9 114.8 %reduce-scatter.4.cloned.1.call-start = ((), (), s32[]{:S(2)}) async-start(), calls=%async_computation.10 | async-start | bytes 2228224 | tf_op jit(solution)/shard_map/reduce_scatter | solution.py:112
  685.3 193.2 %reduce-scatter.6.cloned.1.call-start = ((), (), s32[]{:S(2)}) async-start(), calls=%async_computation.13 | async-start | bytes 2228224 | tf_op jit(solution)/shard_map/reduce_scatter | solution.py:115
  722.9 241.2 %reduce-scatter.8.cloned.1.call-start = ((), (), s32[]{:S(2)}) async-start(), calls=%async_computation.14 | async-start | bytes 4456448 | tf_op jit(solution)/shard_map/reduce_scatter | solution.py:123
  723.9 3.6 copy-start
Sparse Core Ops, SparseCore 0:
  11.0 55.3 all-gather.11
  68.1 102.6 all-gather.13
  173.9 66.1 all-gather.19
  241.7 111.7 all-gather.17
  355.1 108.0 all-gather.9
  466.1 58.3 all-gather.21
  526.3 111.7 all-gather.15
  644.1 34.5 all-reduce.6
  681.9 34.9 all-reduce.8
  720.3 75.4 reduce-scatter.3
  799.7 78.6 reduce-scatter.5
  881.9 82.1 reduce-scatter.7
where the time goes:
time: 973 us
  waiting for transfers between devices  843 us (87%)
  blocking collectives  49.7 us (5%)
  matrix products  36.1 us (4%)
  local copies, waits for them, and re-layouts  15.7 us (2%)
  between operations  14.5 us (1%)
    all_gather x1, waiting for transfers between devices, per_device(): wo_full = lax.all_gather(w_out, 'group', axis=1, tiled=True)  113 us
    all_gather x1, waiting for transfers between devices, per_device(): lax.all_gather(w_key, 'group', axis=0, tiled=True)  109 us
    all_gather x1, waiting for transfers between devices, per_device(): lax.all_gather(w_value, 'group', axis=0, tiled=True)  105 us
    reduce_scatter x1, waiting for transfers between devices, per_device(): lax.psum_scatter(neigh_term.astype(jnp.bfloat16), 'mp', scatter_dimension...  84 us
    reduce_scatter x1, waiting for transfers between devices, per_device(): lax.psum_scatter(hid_term.astype(jnp.bfloat16), 'mp', scatter_dimension=1...  81.1 us
    all_gather x1, waiting for transfers between devices, per_device(): lax.all_gather(grad_rows, 'mp', axis=1, tiled=True)  65.6 us
    reduce_scatter x1, waiting for transfers between devices, per_device(): lax.psum_scatter(out_term.astype(jnp.bfloat16), 'mp', scatter_dimension=1...  64.9 us
    all_gather x1, waiting for transfers between devices, per_device(): neighbours = lax.all_gather(own_cols, 'mp', axis=1, tiled=True)  61.3 us
  transfers between devices with their start and end apart: 13, of which 12 were waited for; matrix products, arithmetic and copies ran while one was open for 5% of the time, Pallas kernels for 0%

commit v1 on v0

--- a/solution.py
+++ b/solution.py
@@ -55,7 +55,12 @@
         - 1
     )
     own_cols = recv_buf.reshape(owners * cap, -1)[own_owner * cap + own_rank]
-    neighbours = lax.all_gather(own_cols, "mp", axis=1, tiled=True)
+    ring = [own_cols]
+    for hop in range(15):
+        ring.append(lax.ppermute(ring[-1], "mp", [(dev, (dev + 1) % 16) for dev in range(16)]))
+    neighbours = jnp.roll(
+        jnp.concatenate(ring[::-1], axis=1), (lax.axis_index("mp") + 1) * ring[0].shape[1], axis=1
+    )
     wq_full, wk_full, wv_full = (
         lax.all_gather(w_query, "group", axis=0, tiled=True),
         lax.all_gather(w_key, "group", axis=0, tiled=True),

time: 973 us -> 919 us (0.945)
  waiting for transfers between devices: 843 us -> 757 us
  local copies, waits for them, and re-layouts: 15.7 us -> 45.3 us
    ppermute x0 -> x15, waiting for transfers between devices: none -> 130 us  [per_device(): lax.ppermute(ring[-1], 'mp', [(dev, (dev + 1) % 16) for dev in range(16)])]
    all_gather x1, waiting for transfers between devices: 65.6 us -> 3.02 us  [per_device(): lax.all_gather(grad_rows, 'mp', axis=1, tiled=True)]
    all_gather x1 -> x0, waiting for transfers between devices: 61.3 us -> none  [per_device(): neighbours = lax.all_gather(own_cols, 'mp', axis=1, tiled=True)]
    all_gather x1, waiting for transfers between devices: 60.2 us -> 0.01 us  [per_device(): lax.all_gather(w_query, 'group', axis=0, tiled=True)]
    all_gather x1, waiting for transfers between devices: 109 us -> 75.1 us  [per_device(): lax.all_gather(w_key, 'group', axis=0, tiled=True)]
    unnamed x7 -> x40, local copies, waits for them, and re-layouts: 0.01 us -> 29 us
  transfers between devices with their start and end apart: 13 -> 27, of which waited for: 12 -> 24; matrix products, arithmetic and copies ran while one was open for 5% -> 9% of each run, Pallas kernels for 0% -> 0%
where the time goes in v1:
time: 919 us; the launch traced here: 918 us
  waiting for transfers between devices  757 us (82%)
  blocking collectives  49.7 us (5%)
  local copies, waits for them, and re-layouts  45.3 us (5%)
  matrix products  36.1 us (4%)
  between operations  14.2 us (2%)
    ppermute x15, waiting for transfers between devices, per_device(): lax.ppermute(ring[-1], 'mp', [(dev, (dev + 1) % 16) for dev in range(16)])  130 us
    all_gather x1, waiting for transfers between devices, per_device(): wo_full = lax.all_gather(w_out, 'group', axis=1, tiled=True)  117 us
    all_gather x1, waiting for transfers between devices, per_device(): lax.all_gather(w_value, 'group', axis=0, tiled=True)  95.9 us
    reduce_scatter x1, waiting for transfers between devices, per_device(): lax.psum_scatter(neigh_term.astype(jnp.bfloat16), 'mp', scatter_dimension...  84.1 us
    reduce_scatter x1, waiting for transfers between devices, per_device(): lax.psum_scatter(hid_term.astype(jnp.bfloat16), 'mp', scatter_dimension=1...  81 us
    all_gather x1, waiting for transfers between devices, per_device(): lax.all_gather(w_key, 'group', axis=0, tiled=True)  75.1 us
    reduce_scatter x1, waiting for transfers between devices, per_device(): lax.psum_scatter(out_term.astype(jnp.bfloat16), 'mp', scatter_dimension=1...  65 us
    all_gather x1, blocking collectives, per_device(): lax.all_gather(flat_ids.astype(jnp.float32), ('dp', 'group'), axis=0, til...  40.9 us
  transfers between devices with their start and end apart: 27, of which 24 were waited for; matrix products, arithmetic and copies ran while one was open for 9% of the time, Pallas kernels for 0%

profile of v1, /device:TPU:2, one launch (start us, length us, event | category | flops | bytes accessed | tf_op | source)
XLA Modules:
  0.0 917.9 jit_solution(3645485150476098056)
XLA Ops:
  9.6 0.9 slice.32
  12.5 40.9 %all-gather = f32[16,1,256]{2,1,0:T(1,128)S(1)} all-gather(f32[1,1,256]{2,1,0:T(1,128)S(1)} %bitcast.105), channel_id=1, replica_groups=mesh['dp'=8,'mp'=16,'group'=2] {'dp','group'}, dimensions={0}, use_global_device_ids=true | all-gather | bytes 17408 | tf_op jit(solution)/shard_map/all_gather | solution.py:39
  54.9 7.9 gather_fusion
  62.8 5.9 all-to-all-start
  70.3 37.5 %all-to-all-done = bf16[16,64,512]{2,1,0:T(8,128)(2,1)S(1)} async-done(((bf16[16,64,512]{2,1,0:T(8,128)(2,1)}), bf16[16,64,512]{2,1,0:T(8,128)(2,1)S(1)}, u32[]{:S(2)}, u32[]{:S(2)}) %all-to-all-start) | async-done | bytes 1048608 | tf_op jit(solution)/shard_map/all_to_all | solution.py:50
  107.8 1.2 gather_fusion.1
  108.9 1.7 collective-permute-start
  110.6 6.9 collective-permute-done
  117.5 8.5 collective-permute-done.1
  126.0 8.7 collective-permute-done.2
  134.7 9.4 %collective-permute-done.3 = bf16[256,512]{1,0:T(8,128)(2,1)S(1)} collective-permute-done((bf16[256,512]{1,0:T(8,128)(2,1)S(1)}, bf16[256,512]{1,0:T(8,128)(2,1)S(1)}, u32[]{:S(2)}, u32[]{:S(2)}) %collective-permute-start.3) | collective-permute-done | bytes 262176 | tf_op jit(solution)/shard_map/ppermute | solution.py:60
  144.1 10.1 %collective-permute-done.4 = bf16[256,512]{1,0:T(8,128)(2,1)S(1)} collective-permute-done((bf16[256,512]{1,0:T(8,128)(2,1)S(1)}, bf16[256,512]{1,0:T(8,128)(2,1)S(1)}, u32[]{:S(2)}, u32[]{:S(2)}) %collective-permute-start.4) | collective-permute-done | bytes 262176 | tf_op jit(solution)/shard_map/ppermute | solution.py:60
  154.2 11.0 %collective-permute-done.5 = bf16[256,512]{1,0:T(8,128)(2,1)S(1)} collective-permute-done((bf16[256,512]{1,0:T(8,128)(2,1)S(1)}, bf16[256,512]{1,0:T(8,128)(2,1)S(1)}, u32[]{:S(2)}, u32[]{:S(2)}) %collective-permute-start.5) | collective-permute-done | bytes 262176 | tf_op jit(solution)/shard_map/ppermute | solution.py:60
  165.2 10.9 %collective-permute-done.6 = bf16[256,512]{1,0:T(8,128)(2,1)S(1)} collective-permute-done((bf16[256,512]{1,0:T(8,128)(2,1)S(1)}, bf16[256,512]{1,0:T(8,128)(2,1)S(1)}, u32[]{:S(2)}, u32[]{:S(2)}) %collective-permute-start.6) | collective-permute-done | bytes 262176 | tf_op jit(solution)/shard_map/ppermute | solution.py:60
  176.0 10.1 %collective-permute-done.7 = bf16[256,512]{1,0:T(8,128)(2,1)S(1)} collective-permute-done((bf16[256,512]{1,0:T(8,128)(2,1)S(1)}, bf16[256,512]{1,0:T(8,128)(2,1)S(1)}, u32[]{:S(2)}, u32[]{:S(2)}) %collective-permute-start.7) | collective-permute-done | bytes 262176 | tf_op jit(solution)/shard_map/ppermute | solution.py:60
  186.1 9.2 %collective-permute-done.8 = bf16[256,512]{1,0:T(8,128)(2,1)S(1)} collective-permute-done((bf16[256,512]{1,0:T(8,128)(2,1)S(1)}, bf16[256,512]{1,0:T(8,128)(2,1)S(1)}, u32[]{:S(2)}, u32[]{:S(2)}) %collective-permute-start.8) | collective-permute-done | bytes 262176 | tf_op jit(solution)/shard_map/ppermute | solution.py:60
  195.4 8.5 collective-permute-done.9
  203.9 8.9 collective-permute-done.10
  212.8 8.9 collective-permute-done.11
  221.8 9.0 collective-permute-done.12
  230.8 3.5 convolution_convert_fusion.4
  234.4 9.6 %collective-permute-done.13 = bf16[256,512]{1,0:T(8,128)(2,1)} collective-permute-done((bf16[256,512]{1,0:T(8,128)(2,1)}, bf16[256,512]{1,0:T(8,128)(2,1)}, u32[]{:S(2)}, u32[]{:S(2)}) %collective-permute-start.13) | collective-permute-done | bytes 262176 | tf_op jit(solution)/shard_map/ppermute | solution.py:60
  244.0 3.0 all-gather.18.cloned.1.call-done
  247.0 117.2 %all-gather.16.cloned.1.call-done = bf16[256,8192]{1,0:T(8,128)(2,1)} async-done(((bf16[256,4096]{1,0:T(8,128)(2,1)}), bf16[256,8192]{1,0:T(8,128)(2,1)}) %all-gather.16.cloned.1.call-update) | async-done | bytes 4194320 | tf_op jit(solution)/shard_map/all_gather | solution.py:71
  364.2 4.4 convolution_convert_fusion.3
  369.2 1.7 constant_dynamic-update-slice_fusion.31
  370.9 1.7 constant_dynamic-update-slice_fusion.30
  372.6 1.8 constant_dynamic-update-slice_fusion.29
  384.1 1.7 constant_dynamic-update-slice_fusion.15
  385.8 1.7 constant_dynamic-update-slice_fusion.14
  387.5 1.7 constant_dynamic-update-slice_fusion.13
  398.9 75.1 %all-gather.14.cloned.1.call-done = bf16[8192,256]{1,0:T(8,128)(2,1)} async-done(((bf16[4096,256]{1,0:T(8,128)(2,1)}), bf16[8192,256]{1,0:T(8,128)(2,1)}) %all-gather.14.cloned.1.call-update) | async-done | bytes 4194320 | tf_op jit(solution)/shard_map/all_gather | solution.py:66
  474.0 4.7 fusion.9
  479.0 8.8 psum.22
  487.9 95.9 %all-gather.8.cloned.1.call-done = bf16[8192,256]{1,0:T(8,128)(2,1)} async-done(((bf16[4096,256]{1,0:T(8,128)(2,1)}), bf16[8192,256]{1,0:T(8,128)(2,1)}) %all-gather.8.cloned.1.call-update) | async-done | bytes 4194320 | tf_op jit(solution)/shard_map/all_gather | solution.py:67
  583.8 4.7 fusion.6
  589.4 34.7 %all-reduce.7.cloned.1.call-done = f32[2,64,2,128]{3,1,2,0:T(8,128)} async-done(((f32[2,64,2,128]{3,1,2,0:T(8,128)}), f32[2,64,2,128]{3,1,2,0:T(8,128)}) %all-reduce.7.cloned.1.call-update) | async-done | bytes 131088 | tf_op jit(solution)/shard_map/psum | solution.py:90
  624.1 1.1 multiply_reduce_fusion
  626.4 4.2 convolution_convert_fusion.1
  630.7 31.5 %all-reduce.9.cloned.1.call-done = f32[2,64,2,128]{3,1,2,0:T(8,128)} async-done(((f32[2,64,2,128]{3,1,2,0:T(8,128)}), f32[2,64,2,128]{3,1,2,0:T(8,128)}) %all-reduce.9.cloned.1.call-update) | async-done | bytes 131088 | tf_op jit(solution)/shard_map/psum | solution.py:104
  662.3 0.9 multiply_convert_fusion
  663.3 5.0 convolution_convert_fusion
  669.4 3.6 fusion.21
  673.0 3.2 fusion
  676.3 65.0 %reduce-scatter.4.cloned.1.call-done = bf16[128,512]{1,0:T(8,128)(2,1)} async-done(((bf16[128,8192]{1,0:T(8,128)(2,1)}), bf16[128,512]{1,0:T(8,128)(2,1)}) %reduce-scatter.4.cloned.1.call-update) | async-done | bytes 131088 | tf_op jit(solution)/shard_map/reduce_scatter | solution.py:117
  742.9 81.0 %reduce-scatter.6.cloned.1.call-done = bf16[128,512]{1,0:T(8,128)(2,1)} async-done(((bf16[128,8192]{1,0:T(8,128)(2,1)}), bf16[128,512]{1,0:T(8,128)(2,1)}) %reduce-scatter.6.cloned.1.call-update) | async-done | bytes 131088 | tf_op jit(solution)/shard_map/reduce_scatter | solution.py:120
  825.5 84.1 %reduce-scatter.8.cloned.1.call-done = bf16[256,512]{1,0:T(8,128)(2,1)} async-done(((bf16[256,8192]{1,0:T(8,128)(2,1)}), bf16[256,512]{1,0:T(8,128)(2,1)}) %reduce-scatter.8.cloned.1.call-update) | async-done | bytes 262160 | tf_op jit(solution)/shard_map/reduce_scatter | solution.py:128
  909.6 1.8 convert.9
  (123 shorter events, 34.4 us)
Async XLA Ops:
  7.2 223.6 %all-gather.10.cloned.1.call-start = ((), (), s32[]{:S(2)}) async-start(), calls=%async_computation.5 | async-start | bytes 2228224 | tf_op jit(solution)/shard_map/all_gather | solution.py:31
  8.8 222.0 %all-gather.12.cloned.1.call-start = ((), (), s32[]{:S(2)}) async-start(), calls=%async_computation.6 | async-start | bytes 6291456 | tf_op jit(solution)/shard_map/all_gather | solution.py:65
  9.6 59.7 %copy-start.2 = (s32[2,1,128]{2,1,0:T(1,128)S(1)}, s32[2,1,128]{2,1,0:T(1,128)}, u32[]{:S(2)}) copy-start(s32[2,1,128]{2,1,0:T(1,128)} %param.10) | copy-start | bytes 3076
  9.6 237.4 %all-gather.18.cloned.1.call-start = ((), (), s32[]{:S(2)}) async-start(), calls=%async_computation.11 | async-start | bytes 2228224 | tf_op jit(solution)/shard_map/all_gather | solution.py:32
  11.2 353.0 %all-gather.16.cloned.1.call-start = ((), (), s32[]{:S(2)}) async-start(), calls=%async_computation.9 | async-start | bytes 6291456 | tf_op jit(solution)/shard_map/all_gather | solution.py:71
  54.9 166.9 %copy-start.3 = (s32[2]{0:T(128)S(1)}, s32[2]{0:T(128)}, u32[]{:S(2)}) copy-start(s32[2]{0:T(128)} %param.11) | copy-start | bytes 28
  62.8 45.0 %all-to-all-start = ((bf16[16,64,512]{2,1,0:T(8,128)(2,1)}), bf16[16,64,512]{2,1,0:T(8,128)(2,1)S(1)}, u32[]{:S(2)}, u32[]{:S(2)}) async-start(bf16[16,64,512]{2,1,0:T(8,128)(2,1)} %bitcast.4), calls=%async_computation | async-start | bytes 2097152 | tf_op jit(solution)/shard_map/all_to_all | solution.py:50
  68.6 405.3 %all-gather.14.cloned.1.call-start = ((), (), s32[]{:S(2)}) async-start(), calls=%async_computation.7 | async-start | bytes 6291456 | tf_op jit(solution)/shard_map/all_gather | solution.py:66
  69.2 514.6 %all-gather.8.cloned.1.call-start = ((), (), s32[]{:S(2)}) async-start(), calls=%async_computation.4 | async-start | bytes 6291456 | tf_op jit(solution)/shard_map/all_gather | solution.py:67
  108.9 8.6 collective-permute-start
  117.5 8.5 collective-permute-start.1
  126.0 8.7 collective-permute-start.2
  134.7 9.4 %collective-permute-start.3 = (bf16[256,512]{1,0:T(8,128)(2,1)S(1)}, bf16[256,512]{1,0:T(8,128)(2,1)S(1)}, u32[]{:S(2)}, u32[]{:S(2)}) collective-permute-start(bf16[256,512]{1,0:T(8,128)(2,1)S(1)} %collective-permute-done.2), channel_id=1, source_target_pairs={{0,2},{2,4},{4,6},{6,8},{8,10},{10,12},{12,14},{14,16},{16,18},{18... | collective-permute-start | bytes 786440 | tf_op jit(solution)/shard_map/ppermute | solution.py:60
  144.1 10.1 %collective-permute-start.4 = (bf16[256,512]{1,0:T(8,128)(2,1)S(1)}, bf16[256,512]{1,0:T(8,128)(2,1)S(1)}, u32[]{:S(2)}, u32[]{:S(2)}) collective-permute-start(bf16[256,512]{1,0:T(8,128)(2,1)S(1)} %collective-permute-done.3), channel_id=1, source_target_pairs={{0,2},{2,4},{4,6},{6,8},{8,10},{10,12},{12,14},{14,16},{16,18},{18... | collective-permute-start | bytes 786440 | tf_op jit(solution)/shard_map/ppermute | solution.py:60
  154.2 11.0 %collective-permute-start.5 = (bf16[256,512]{1,0:T(8,128)(2,1)S(1)}, bf16[256,512]{1,0:T(8,128)(2,1)S(1)}, u32[]{:S(2)}, u32[]{:S(2)}) collective-permute-start(bf16[256,512]{1,0:T(8,128)(2,1)S(1)} %collective-permute-done.4), channel_id=1, source_target_pairs={{0,2},{2,4},{4,6},{6,8},{8,10},{10,12},{12,14},{14,16},{16,18},{18... | collective-permute-start | bytes 786440 | tf_op jit(solution)/shard_map/ppermute | solution.py:60
  165.2 10.9 %collective-permute-start.6 = (bf16[256,512]{1,0:T(8,128)(2,1)S(1)}, bf16[256,512]{1,0:T(8,128)(2,1)S(1)}, u32[]{:S(2)}, u32[]{:S(2)}) collective-permute-start(bf16[256,512]{1,0:T(8,128)(2,1)S(1)} %collective-permute-done.5), channel_id=1, source_target_pairs={{0,2},{2,4},{4,6},{6,8},{8,10},{10,12},{12,14},{14,16},{16,18},{18... | collective-permute-start | bytes 786440 | tf_op jit(solution)/shard_map/ppermute | solution.py:60
  176.0 10.1 %collective-permute-start.7 = (bf16[256,512]{1,0:T(8,128)(2,1)S(1)}, bf16[256,512]{1,0:T(8,128)(2,1)S(1)}, u32[]{:S(2)}, u32[]{:S(2)}) collective-permute-start(bf16[256,512]{1,0:T(8,128)(2,1)S(1)} %collective-permute-done.6), channel_id=1, source_target_pairs={{0,2},{2,4},{4,6},{6,8},{8,10},{10,12},{12,14},{14,16},{16,18},{18... | collective-permute-start | bytes 786440 | tf_op jit(solution)/shard_map/ppermute | solution.py:60
  186.1 9.2 %collective-permute-start.8 = (bf16[256,512]{1,0:T(8,128)(2,1)S(1)}, bf16[256,512]{1,0:T(8,128)(2,1)S(1)}, u32[]{:S(2)}, u32[]{:S(2)}) collective-permute-start(bf16[256,512]{1,0:T(8,128)(2,1)S(1)} %collective-permute-done.7), channel_id=1, source_target_pairs={{0,2},{2,4},{4,6},{6,8},{8,10},{10,12},{12,14},{14,16},{16,18},{18... | collective-permute-start | bytes 786440 | tf_op jit(solution)/shard_map/ppermute | solution.py:60
  195.4 8.5 collective-permute-start.9
  203.8 9.0 collective-permute-start.10
  212.8 8.9 collective-permute-start.11
  221.7 9.1 collective-permute-start.12
  221.8 402.4 %all-reduce.7.cloned.1.call-start = ((), (), s32[]{:S(2)}) async-start(), calls=%async_computation.8 | async-start | bytes 262144 | tf_op jit(solution)/shard_map/psum | solution.py:90
  230.8 13.2 %collective-permute-start.13 = (bf16[256,512]{1,0:T(8,128)(2,1)}, bf16[256,512]{1,0:T(8,128)(2,1)}, u32[]{:S(2)}, u32[]{:S(2)}) collective-permute-start(bf16[256,512]{1,0:T(8,128)(2,1)} %collective-permute-done.12), channel_id=1, source_target_pairs={{0,2},{2,4},{4,6},{6,8},{8,10},{10,12},{12,14},{14,16},{16,18},{18... | collective-permute-start | bytes 786440 | tf_op jit(solution)/shard_map/ppermute | solution.py:60
  244.0 125.2 %collective-permute-start.14 = (bf16[256,512]{1,0:T(8,128)(2,1)}, bf16[256,512]{1,0:T(8,128)(2,1)}, u32[]{:S(2)}, u32[]{:S(2)}) collective-permute-start(bf16[256,512]{1,0:T(8,128)(2,1)} %collective-permute-done.13), channel_id=1, source_target_pairs={{0,2},{2,4},{4,6},{6,8},{8,10},{10,12},{12,14},{14,16},{16,18},{18... | collective-permute-start | bytes 786440 | tf_op jit(solution)/shard_map/ppermute | solution.py:60
  398.9 225.2 %copy-start.1 = (bf16[2,64,2,128]{3,2,1,0:T(2,128)(2,1)S(1)}, bf16[2,64,2,128]{3,2,1,0:T(2,128)(2,1)}, u32[]{:S(2)}) copy-start(bf16[2,64,2,128]{3,2,1,0:T(2,128)(2,1)} %reshape.264) | copy-start | bytes 196612
  589.4 72.9 %all-reduce.9.cloned.1.call-start = ((), (), s32[]{:S(2)}) async-start(), calls=%async_computation.12 | async-start | bytes 262144 | tf_op jit(solution)/shard_map/psum | solution.py:104
  626.3 115.0 %reduce-scatter.4.cloned.1.call-start = ((), (), s32[]{:S(2)}) async-start(), calls=%async_computation.10 | async-start | bytes 2228224 | tf_op jit(solution)/shard_map/reduce_scatter | solution.py:117
  630.7 193.2 %reduce-scatter.6.cloned.1.call-start = ((), (), s32[]{:S(2)}) async-start(), calls=%async_computation.13 | async-start | bytes 2228224 | tf_op jit(solution)/shard_map/reduce_scatter | solution.py:120
  668.3 241.3 %reduce-scatter.8.cloned.1.call-start = ((), (), s32[]{:S(2)}) async-start(), calls=%async_computation.14 | async-start | bytes 4456448 | tf_op jit(solution)/shard_map/reduce_scatter | solution.py:128
  669.4 3.6 copy-start
Sparse Core Ops, SparseCore 0:
  11.0 55.3 all-gather.9
  68.1 102.5 all-gather.11
  173.7 73.2 all-gather.17
  248.7 115.4 all-gather.15
  365.8 108.0 all-gather.13
  475.6 108.0 all-gather.7
  589.5 34.5 all-reduce.6
  627.3 34.9 all-reduce.8
  665.8 75.4 reduce-scatter.3
  745.1 78.6 reduce-scatter.5
  827.5 82.0 reduce-scatter.7
